TPU v7x, 256 devices: a whole 4x4x8 slice. The times are simulated.
256 devices in a mesh: dp: 4 (over x), expert: 64 (over z, y, core).
Axes of the slice: x: 4, y: 4, z: 8, core: 2. Of those that a mesh axis runs over, the one named last changes fastest.
Arguments:
- cell_table: bfloat16 [524288, 256], P(('dp', 'expert')), may hold values from -6 to 6
- sample_index: int32 [262144], P(('dp', 'expert')), may hold values from 0 to 2047
- region: int32 [262144, 1], P(('dp', 'expert')), may hold values from 0 to 63; in each aligned block of 1024 rows (0 to 1023, 1024 to 2047, ...) at most 32 rows name the same one
- targets: bfloat16 [262144, 256], P(('dp', 'expert')), may hold values from -6 to 6
- trunk_weight: bfloat16 [256, 256], replicated, may hold values from -0.375 to 0.375
- expert_params: float32 [64, 2, 256, 2048], P('expert', None, None, 'dp'), may hold values from -0.375 to 0.375
- first_moment: float32 [64, 2, 256, 2048], P('expert', None, None, 'dp'), may hold values from -4 to 4
- second_moment: float32 [64, 2, 256, 2048], P('expert', None, None, 'dp'), may hold values from 0.05 to 1
Outputs:
- trunk_grad: float32 [256, 256], replicated
- row_loss: float32 [262144], P(('dp', 'expert'))
- new_params: float32 [64, 2, 256, 2048], P('expert', None, None, 'dp')
- new_first: float32 [64, 2, 256, 2048], P('expert', None, None, 'dp')
- new_second: float32 [64, 2, 256, 2048], P('expert', None, None, 'dp')
Inputs may be any that keep to these rules, and one draw needn't show every extreme that they name: In the 1024 rows of one device no region is named more than 32 times; some region exactly 32 times. `sample_index`: indexes the rows of the same device's block of cell_table.
All inputs are finite; a program needn't handle non-finite values.
Results may differ from a plain program's by a relative error of at most 0.0044.
Values may be sent and summed in bfloat16 or wider, within the bound.
A program may use at most 128 MiB of HBM per device.

v0:
```python
import jax
import jax.numpy as jnp
from jax import lax
from jax.sharding import PartitionSpec as P

loss_scale = 1.0 / 32.0
beta_one = 0.9
beta_two = 0.999
learn_rate = 0.05
adam_eps = 1e-08
adam_step = 10


def silu_slope(values):
    sigma = jax.nn.sigmoid(values)
    return sigma * (1.0 + values * (1.0 - sigma))


def expert_forward(arrived, w_up, w_down):
    up_pre = jnp.dot(arrived, w_up, preferred_element_type=jnp.float32)
    hidden = jax.nn.silu(up_pre).astype(jnp.bfloat16)
    predicted = lax.dot_general(
        hidden, w_down, (((1,), (1,)), ((), ())), preferred_element_type=jnp.float32
    )
    return (up_pre, hidden, predicted)


def expert_backward(arrived, up_pre, hidden, scaled_error, w_up, w_down):
    grad_down = lax.dot_general(
        scaled_error, hidden, (((0,), (0,)), ((), ())), preferred_element_type=jnp.float32
    )
    hidden_grad = jnp.dot(scaled_error, w_down, preferred_element_type=jnp.float32)
    pre_grad = (hidden_grad * silu_slope(up_pre)).astype(jnp.bfloat16)
    grad_up = lax.dot_general(
        arrived, pre_grad, (((0,), (0,)), ((), ())), preferred_element_type=jnp.float32
    )
    input_grad = lax.dot_general(
        pre_grad, w_up, (((1,), (1,)), ((), ())), preferred_element_type=jnp.float32
    ).astype(jnp.bfloat16)
    return (grad_up, grad_down, input_grad)


def error_terms(predicted, target):
    errors = predicted - target.astype(jnp.float32)
    losses = jnp.sum(errors * errors, axis=1) * (0.5 * loss_scale)
    return (losses, (errors * loss_scale).astype(jnp.bfloat16))


def adam_update(params, first, second, grads):
    first_new = beta_one * first + (1.0 - beta_one) * grads
    second_new = beta_two * second + (1.0 - beta_two) * grads * grads
    first_hat = first_new / (1.0 - beta_one**adam_step)
    second_hat = second_new / (1.0 - beta_two**adam_step)
    return (
        params - learn_rate * first_hat / (jnp.sqrt(second_hat) + adam_eps),
        first_new,
        second_new,
    )


def on_device(
    cell_table,
    sample_index,
    region,
    targets,
    trunk_weight,
    expert_params,
    first_moment,
    second_moment,
):
    rows = sample_index.shape[0]
    width = cell_table.shape[1]
    experts = lax.axis_size("expert")
    capacity = 2 * rows // experts
    features = jnp.take(cell_table, sample_index, axis=0)
    trunk_pre = jnp.dot(features, trunk_weight, preferred_element_type=jnp.float32)
    trunk_out = (features.astype(jnp.float32) + jax.nn.silu(trunk_pre)).astype(jnp.bfloat16)
    routed = region[:, 0]
    onehot = (routed[:, None] == jnp.arange(experts, dtype=jnp.int32)[None, :]).astype(jnp.int32)
    slots = jnp.sum(jnp.cumsum(onehot, axis=0) * onehot, axis=1) - 1
    places = routed * capacity + slots

    def pack(values):
        empty = jnp.zeros((experts * capacity,) + values.shape[1:], values.dtype)
        return empty.at[places].set(values).reshape((experts, capacity) + values.shape[1:])

    gathered = lax.all_gather(expert_params.astype(jnp.bfloat16), "dp", axis=3, tiled=True)
    w_up = gathered[0, 0]
    w_down = gathered[0, 1]
    arrived = lax.all_to_all(
        pack(trunk_out), "expert", split_axis=0, concat_axis=0, tiled=True
    ).reshape(-1, width)
    up_pre, hidden, predicted = expert_forward(arrived, w_up, w_down)
    returned = lax.all_to_all(
        predicted.reshape(experts, capacity, width),
        "expert",
        split_axis=0,
        concat_axis=0,
        tiled=True,
    )
    row_loss, row_error = error_terms(returned.reshape(-1, width)[places], targets)
    error_there = lax.all_to_all(
        pack(row_error), "expert", split_axis=0, concat_axis=0, tiled=True
    ).reshape(-1, width)
    grad_up, grad_down, input_grad = expert_backward(
        arrived, up_pre, hidden, error_there, w_up, w_down
    )
    back_grad = lax.all_to_all(
        input_grad.reshape(experts, capacity, width),
        "expert",
        split_axis=0,
        concat_axis=0,
        tiled=True,
    )
    row_grad = back_grad.reshape(-1, width)[places]
    trunk_slope = (row_grad.astype(jnp.float32) * silu_slope(trunk_pre)).astype(jnp.bfloat16)
    trunk_local = lax.dot_general(
        features, trunk_slope, (((0,), (0,)), ((), ())), preferred_element_type=jnp.float32
    )
    trunk_grad = lax.psum(trunk_local, ("dp", "expert"))
    grads = jnp.stack([grad_up, grad_down])[None]
    grad_shard = lax.psum_scatter(grads, "dp", scatter_dimension=3, tiled=True)
    new_params, new_first, new_second = adam_update(
        expert_params, first_moment, second_moment, grad_shard
    )
    return (trunk_grad, row_loss, new_params, new_first, new_second)


def solution(mesh):
    placed = (
        P(("dp", "expert"), None),
        P(("dp", "expert")),
        P(("dp", "expert"), None),
        P(("dp", "expert"), None),
        P(),
        P("expert", None, None, "dp"),
        P("expert", None, None, "dp"),
        P("expert", None, None, "dp"),
    )
    return jax.shard_map(
        on_device,
        mesh=mesh,
        in_specs=placed,
        out_specs=(
            P(),
            P(("dp", "expert")),
            P("expert", None, None, "dp"),
            P("expert", None, None, "dp"),
            P("expert", None, None, "dp"),
        ),
        check_vma=False,
    )
```

profile of v0, /device:TPU:2, one launch (start us, length us, event | category | flops | bytes accessed | tf_op | source)
XLA Modules:
  0.0 533.0 jit_solution(5352181415112622577)
XLA Ops:
  7.3 2.2 convert_element_type.38
  9.5 0.7 fusion.15
  10.2 18.0 %reduce-window.6 = s32[64,8,128]{2,1,0:T(8,128)S(1)} reduce-window(s32[64,8,128]{2,1,0:T(8,128)S(1)} %fusion.15, s32[]{:T(128)} %constant.18.clone.1), window={size=1x1x128 pad=0_0x0_0x127_0}, to_apply=%region_0.1 | reduce-window | flops 8323072 | bytes 524292 | tf_op jit(solution)/shard_map/reduce-window
  28.7 0.7 fusion.16
  29.4 3.9 gather_fusion
  33.5 0.4 fusion.18
  33.9 6.0 %scatter_custom_fusion = bf16[2048,256]{1,0:T(8,128)(2,1)S(1)} fusion(s32[1024]{0:T(1024)S(1)} %bitcast.70, bf16[]{:T(256)} %constant.22.clone.1, f32[1024,256]{1,0:T(8,128)S(1)} %fusion.18, f32[]{:T(128)} %constant.15.clone.1, bf16[1024,256]{1,0:T(8,128)(2,1)S(1)} %gather_fusion, pred[1024]{0:T(1024)(128)(4,1)S(1)} %compare_and_fusion), kind=kCustom, calls=%fused_computation.32 | custom fusion | flops 2097152 | bytes 2622470 | tf_op jit(solution)/shard_map/scatter | solution.py:85
  39.9 40.8 %all_to_all.20 = bf16[64,32,256]{2,1,0:T(8,128)(2,1)S(1)} all-to-all(bf16[64,32,256]{2,1,0:T(8,128)(2,1)S(1)} %bitcast.64), channel_id=1, replica_groups=mesh['dp'=4,'expert'=64] {'expert'}, dimensions={0} | all-to-all | bytes 2097152 | tf_op jit(solution)/shard_map/all_to_all | solution.py:90
  80.7 9.8 %multiply_convert_fusion.1 = (bf16[2048,2048]{1,0:T(8,128)(2,1)S(1)}, f32[2048,2048]{1,0:T(8,128)}) fusion(bf16[2048,256]{1,0:T(8,128)(2,1)S(1)} %bitcast.59, bf16[1,2,256,2048]{3,2,1,0:T(8,128)(2,1)} %all-gather.2.cloned.1.call-done), kind=kOutput, calls=%fused_computation.6 | convolution fusion | flops 2168455168 | bytes 27262976 | tf_op jit(solution)/shard_map/dot_general | solution.py:20
  90.5 3.2 copy-done.2
  93.8 3.8 fusion.1
  97.6 5.6 %all-to-all-start.1 = ((f32[64,32,256]{2,1,0:T(8,128)}), f32[64,32,256]{2,1,0:T(8,128)S(1)}, u32[]{:S(2)}, u32[]{:S(2)}) async-start(f32[64,32,256]{2,1,0:T(8,128)} %fusion.1), calls=%async_computation.1 | async-start | bytes 4194304 | tf_op jit(solution)/shard_map/all_to_all | solution.py:94
  103.1 0.2 reduce-scatter.2.cloned.1.call-start
  103.4 51.1 %all-to-all-done.1 = f32[64,32,256]{2,1,0:T(8,128)S(1)} async-done(((f32[64,32,256]{2,1,0:T(8,128)}), f32[64,32,256]{2,1,0:T(8,128)S(1)}, u32[]{:S(2)}, u32[]{:S(2)}) %all-to-all-start.1) | async-done | bytes 2097184 | tf_op jit(solution)/shard_map/all_to_all | solution.py:94
  154.5 3.5 gather_fusion.1
  157.9 5.7 %scatter_custom_fusion.1 = bf16[2048,256]{1,0:T(8,128)(2,1)S(1)} fusion(s32[1024]{0:T(1024)S(1)} %bitcast.72, f32[1024,256]{1,0:T(8,128)S(1)} %gather_fusion.1, bf16[1024,256]{1,0:T(8,128)(2,1)} %param.11, f32[]{:T(128)} %constant.16.clone.1, bf16[]{:T(256)} %constant.22.clone.1), kind=kCustom, calls=%fused_computation.29 | custom fusion | flops 1048576 | bytes 2621446 | tf_op jit(solution)/shard_map/scatter | solution.py:85
  163.7 34.0 %all_to_all.21 = bf16[64,32,256]{2,1,0:T(8,128)(2,1)S(1)} all-to-all(bf16[64,32,256]{2,1,0:T(8,128)(2,1)S(1)} %bitcast.63), channel_id=1, replica_groups=mesh['dp'=4,'expert'=64] {'expert'}, dimensions={0} | all-to-all | bytes 2097152 | tf_op jit(solution)/shard_map/all_to_all | solution.py:102
  197.7 5.9 %convolution_bitcast_fusion = f32[1,256,2048]{2,1,0:T(8,128)S(1)} fusion(bf16[2048,256]{1,0:T(8,128)(2,1)S(1)} %bitcast.61, bf16[2048,2048]{1,0:T(8,128)(2,1)} %copy-done.2), kind=kOutput, calls=%fused_computation.9 | convolution fusion | flops 2147483648 | bytes 11534336 | tf_op jit(solution)/shard_map/dot_general | solution.py:29
  203.6 10.4 %multiply_convert_fusion = bf16[2048,2048]{1,0:T(8,128)(2,1)S(1)} fusion(f32[2048,2048]{1,0:T(8,128)} %get-tuple-element.9, bf16[2048,256]{1,0:T(8,128)(2,1)S(1)} %bitcast.62, bf16[1,2,256,2048]{3,2,1,0:T(8,128)(2,1)S(1)} %copy-done.14), kind=kOutput, calls=%fused_computation.5 | convolution fusion | flops 2185232384 | bytes 27262976 | tf_op jit(solution)/shard_map/dot_general | solution.py:32
  214.0 3.2 copy-done.3
  217.2 2.3 convolution_bitcast_fusion.1
  219.6 2.2 maximum_bitcast_fusion
  221.8 7.0 %convolution_convert_fusion = bf16[2048,256]{1,0:T(8,128)(2,1)} fusion(bf16[2048,2048]{1,0:T(8,128)(2,1)} %copy-done.3, bf16[1,2,256,2048]{3,2,1,0:T(8,128)(2,1)} %all-gather.2.cloned.1.call-done), kind=kOutput, calls=%fused_computation.11 | convolution fusion | flops 2148007936 | bytes 10485760 | tf_op jit(solution)/shard_map/dot_general | solution.py:37
  228.9 5.7 %all-to-all-start.3 = ((bf16[64,32,256]{2,1,0:T(8,128)(2,1)}), bf16[64,32,256]{2,1,0:T(8,128)(2,1)S(1)}, u32[]{:S(2)}, u32[]{:S(2)}) async-start(bf16[64,32,256]{2,1,0:T(8,128)(2,1)} %bitcast.65), calls=%async_computation.3 | async-start | bytes 2097152 | tf_op jit(solution)/shard_map/all_to_all | solution.py:108
  234.6 0.2 multiply_reduce_fusion
  234.9 0.6 broadcast_multiply_fusion
  235.5 28.0 %all-to-all-done.3 = bf16[64,32,256]{2,1,0:T(8,128)(2,1)S(1)} async-done(((bf16[64,32,256]{2,1,0:T(8,128)(2,1)}), bf16[64,32,256]{2,1,0:T(8,128)(2,1)S(1)}, u32[]{:S(2)}, u32[]{:S(2)}) %all-to-all-start.3) | async-done | bytes 1048608 | tf_op jit(solution)/shard_map/all_to_all | solution.py:108
  263.5 3.9 gather_fusion.2
  267.4 2.7 fusion.12
  270.2 4.3 divide_subtract_fusion
  274.5 250.3 %all-reduce.2.cloned.1.call-done = f32[256,256]{1,0:T(8,128)} async-done(((f32[256,256]{1,0:T(8,128)}), f32[256,256]{1,0:T(8,128)}) %all-reduce.2.cloned.1.call-update) | async-done | bytes 262160 | tf_op jit(solution)/shard_map/psum | solution.py:120
  524.8 1.7 copy.18
  (46 shorter events, 0.8 us)
Async XLA Ops:
  7.2 22.3 %copy-start = (bf16[2048,256]{1,0:T(8,128)(2,1)S(1)}, bf16[2048,256]{1,0:T(8,128)(2,1)}, u32[]{:S(2)}) copy-start(bf16[2048,256]{1,0:T(8,128)(2,1)} %param.8) | copy-start | bytes 3145732
  7.2 26.2 %copy-start.11 = (s32[1024,1]{0,1:T(1,128)S(1)}, s32[1024,1]{0,1:T(1,128)}, u32[]{:S(2)}) copy-start(s32[1024,1]{0,1:T(1,128)} %param.10) | copy-start | bytes 12292
  7.2 26.3 %copy-start.12 = (s32[1024]{0:T(1024)S(1)}, s32[1024]{0:T(1024)}, u32[]{:S(2)}) copy-start(s32[1024]{0:T(1024)} %param.9) | copy-start | bytes 12292
  7.2 26.3 %copy-start.10 = (bf16[256,256]{1,0:T(8,128)(2,1)S(1)}, bf16[256,256]{1,0:T(8,128)(2,1)}, u32[]{:S(2)}) copy-start(bf16[256,256]{1,0:T(8,128)(2,1)} %param.12) | copy-start | bytes 393220
  7.2 73.5 %all-gather.2.cloned.1.call-start = ((), (), s32[]{:S(2)}) async-start(), calls=%async_computation.5 | async-start | bytes 2621440 | tf_op jit(solution)/shard_map/all_gather | solution.py:87
  33.4 57.2 %copy-start.6 = (bf16[1024,256]{1,0:T(8,128)(2,1)}, bf16[1024,256]{1,0:T(8,128)(2,1)S(1)}, u32[]{:S(2)}) copy-start(bf16[1024,256]{1,0:T(8,128)(2,1)S(1)} %gather_fusion) | copy-start | bytes 1572868
  33.9 6.0 %copy-start.8 = (f32[1024,256]{1,0:T(8,128)}, f32[1024,256]{1,0:T(8,128)S(1)}, u32[]{:S(2)}) copy-start(f32[1024,256]{1,0:T(8,128)S(1)} %fusion.18) | copy-start | bytes 3145732
  80.7 9.8 %copy-start.4 = (bf16[64,32,256]{2,1,0:T(8,128)(2,1)}, bf16[64,32,256]{2,1,0:T(8,128)(2,1)S(1)}, u32[]{:S(2)}) copy-start(bf16[64,32,256]{2,1,0:T(8,128)(2,1)S(1)} %all_to_all.20) | copy-start | bytes 3145732
  80.7 13.0 %copy-start.13 = (bf16[1,2,256,2048]{3,2,1,0:T(8,128)(2,1)S(1)}, bf16[1,2,256,2048]{3,2,1,0:T(8,128)(2,1)}, u32[]{:S(2)}) copy-start(bf16[1,2,256,2048]{3,2,1,0:T(8,128)(2,1)} %all-gather.2.cloned.1.call-done) | copy-start | bytes 6291460
  90.5 3.2 copy-start.2
  97.6 56.9 %all-to-all-start.1 = ((f32[64,32,256]{2,1,0:T(8,128)}), f32[64,32,256]{2,1,0:T(8,128)S(1)}, u32[]{:S(2)}, u32[]{:S(2)}) async-start(f32[64,32,256]{2,1,0:T(8,128)} %fusion.1), calls=%async_computation.1 | async-start | bytes 4194304 | tf_op jit(solution)/shard_map/all_to_all | solution.py:94
  103.1 167.0 %reduce-scatter.2.cloned.1.call-start = ((), (), s32[]{:S(2)}) async-start(), calls=%async_computation.7 | async-start | bytes 5242880 | tf_op jit(solution)/shard_map/reduce_scatter | solution.py:122
  197.7 5.9 %copy-start.14 = (bf16[1,2,256,2048]{3,2,1,0:T(8,128)(2,1)S(1)}, bf16[1,2,256,2048]{3,2,1,0:T(8,128)(2,1)}, u32[]{:S(2)}) copy-start(bf16[1,2,256,2048]{3,2,1,0:T(8,128)(2,1)} %all-gather.2.cloned.1.call-done) | copy-start | bytes 6291460
  203.6 13.6 %copy-start.5 = (bf16[64,32,256]{2,1,0:T(8,128)(2,1)S(1)}, bf16[64,32,256]{2,1,0:T(8,128)(2,1)}, u32[]{:S(2)}) copy-start(bf16[64,32,256]{2,1,0:T(8,128)(2,1)} %copy-done.4) | copy-start | bytes 3145732
  214.0 3.2 copy-start.3
  221.8 12.8 %copy-start.9 = (bf16[1024,256]{1,0:T(8,128)(2,1)S(1)}, bf16[1024,256]{1,0:T(8,128)(2,1)}, u32[]{:S(2)}) copy-start(bf16[1024,256]{1,0:T(8,128)(2,1)} %param.11) | copy-start | bytes 1572868
  228.9 38.5 %copy-start.7 = (bf16[1024,256]{1,0:T(8,128)(2,1)S(1)}, bf16[1024,256]{1,0:T(8,128)(2,1)}, u32[]{:S(2)}) copy-start(bf16[1024,256]{1,0:T(8,128)(2,1)} %copy-done.6) | copy-start | bytes 1572868
  228.9 34.6 %all-to-all-start.3 = ((bf16[64,32,256]{2,1,0:T(8,128)(2,1)}), bf16[64,32,256]{2,1,0:T(8,128)(2,1)S(1)}, u32[]{:S(2)}, u32[]{:S(2)}) async-start(bf16[64,32,256]{2,1,0:T(8,128)(2,1)} %bitcast.65), calls=%async_computation.3 | async-start | bytes 2097152 | tf_op jit(solution)/shard_map/all_to_all | solution.py:108
  234.6 290.2 %all-reduce.2.cloned.1.call-start = ((), (), s32[]{:S(2)}) async-start(), calls=%async_computation.6 | async-start | bytes 524288 | tf_op jit(solution)/shard_map/psum | solution.py:120
  263.5 263.0 %copy-start.1 = (bf16[2048,256]{1,0:T(8,128)(2,1)S(1)}, bf16[2048,256]{1,0:T(8,128)(2,1)}, u32[]{:S(2)}) copy-start(bf16[2048,256]{1,0:T(8,128)(2,1)} %param.8) | copy-start | bytes 3145732
Sparse Core Ops, SparseCore 0:
  10.4 35.3 all-gather.1
  222.0 44.4 reduce-scatter.1
  273.4 251.2 all-reduce.1
where the time goes:
time: 533 us
  waiting for transfers between devices  329 us (62%)
  blocking collectives  74.8 us (14%)
  matrix products  42.3 us (8%)
  other arithmetic  40.9 us (8%)
  local copies, waits for them, and re-layouts  19.9 us (4%)
  between operations  14 us (3%)
  starting transfers between devices  11.6 us (2%)
    psum x1, waiting for transfers between devices, on_device(): trunk_grad = lax.psum(trunk_local, ('dp', 'expert'))  250 us
    all_to_all x1, waiting for transfers between devices, on_device(): lax.all_to_all(predicted.reshape(experts, capacity, width), 'expert', spl...  51.1 us
    all_to_all x1, blocking collectives, on_device(): lax.all_to_all(pack(trunk_out), 'expert', split_axis=0, concat_axis=0, ti...  40.8 us
    all_to_all x1, blocking collectives, on_device(): lax.all_to_all(pack(row_error), 'expert', split_axis=0, concat_axis=0, ti...  34 us
    all_to_all x1, waiting for transfers between devices, on_device(): lax.all_to_all(input_grad.reshape(experts, capacity, width), 'expert', sp...  28 us
    another operation x3, other arithmetic  18.2 us
    scatter x2, other arithmetic, pack(): empty.at[places].set(values).reshape((experts, capacity) + values.shape[1:])  11.7 us
  transfers between devices with their start and end apart: 5, of which 3 were waited for; matrix products, arithmetic and copies ran while one was open for 9% of the time, Pallas kernels for 0%

commit v1 on v0

--- a/solution.py
+++ b/solution.py
@@ -117,7 +117,7 @@
     trunk_local = lax.dot_general(
         features, trunk_slope, (((0,), (0,)), ((), ())), preferred_element_type=jnp.float32
     )
-    trunk_grad = lax.psum(trunk_local, ("dp", "expert"))
+    trunk_grad = jnp.sum(lax.all_gather(trunk_local, ("dp", "expert")), axis=0)
     grads = jnp.stack([grad_up, grad_down])[None]
     grad_shard = lax.psum_scatter(grads, "dp", scatter_dimension=3, tiled=True)
     new_params, new_first, new_second = adam_update(

time: 533 us -> 515 us (0.966)
  waiting for transfers between devices: 329 us -> 261 us
  blocking collectives: 74.8 us -> 109 us
  other arithmetic: 40.9 us -> 62.7 us
  starting transfers between devices: 11.6 us -> 6.09 us
    psum x1 -> x0, waiting for transfers between devices: 250 us -> none  [on_device(): trunk_grad = lax.psum(trunk_local, ('dp', 'expert'))]
    all_gather x0 -> x1, waiting for transfers between devices: none -> 210 us  [on_device(): trunk_grad = jnp.sum(lax.all_gather(trunk_local, ('dp', 'expert')), axis=0)]
    all_to_all x0 -> x1, blocking collectives: none -> 34.4 us  [on_device(): lax.all_to_all(input_grad.reshape(experts, capacity, width), 'expert', sp...]
    all_to_all x1 -> x0, waiting for transfers between devices: 28 us -> none  [on_device(): lax.all_to_all(input_grad.reshape(experts, capacity, width), 'expert', sp...]
    reduce_sum x0 -> x1, other arithmetic: none -> 21.8 us  [on_device(): trunk_grad = jnp.sum(lax.all_gather(trunk_local, ('dp', 'expert')), axis=0)]
    all_to_all x1 -> x0, starting transfers between devices: 5.69 us -> none  [on_device(): lax.all_to_all(input_grad.reshape(experts, capacity, width), 'expert', sp...]
  transfers between devices with their start and end apart: 5 -> 4, of which waited for: 3 -> 2; matrix products, arithmetic and copies ran while one was open for 9% -> 10% of each run, Pallas kernels for 0% -> 0%
where the time goes in v1:
time: 515 us; the launch traced here: 514 us
  waiting for transfers between devices  261 us (51%)
  blocking collectives  109 us (21%)
  other arithmetic  62.7 us (12%)
  matrix products  41.5 us (8%)
  local copies, waits for them, and re-layouts  19.3 us (4%)
  between operations  14.1 us (3%)
  starting transfers between devices  6.09 us (1%)
    all_gather x1, waiting for transfers between devices, on_device(): trunk_grad = jnp.sum(lax.all_gather(trunk_local, ('dp', 'expert')), axis=0)  210 us
    all_to_all x1, waiting for transfers between devices, on_device(): lax.all_to_all(predicted.reshape(experts, capacity, width), 'expert', spl...  51.1 us
    all_to_all x1, blocking collectives, on_device(): lax.all_to_all(pack(trunk_out), 'expert', split_axis=0, concat_axis=0, ti...  40.8 us
    all_to_all x1, blocking collectives, on_device(): lax.all_to_all(input_grad.reshape(experts, capacity, width), 'expert', sp...  34.4 us
    all_to_all x1, blocking collectives, on_device(): lax.all_to_all(pack(row_error), 'expert', split_axis=0, concat_axis=0, ti...  34 us
    reduce_sum x1, other arithmetic, on_device(): trunk_grad = jnp.sum(lax.all_gather(trunk_local, ('dp', 'expert')), axis=0)  21.8 us
    another operation x3, other arithmetic  18.2 us
    scatter x2, other arithmetic, pack(): empty.at[places].set(values).reshape((experts, capacity) + values.shape[1:])  11.9 us
  transfers between devices with their start and end apart: 4, of which 2 were waited for; matrix products, arithmetic and copies ran while one was open for 10% of the time, Pallas kernels for 0%

profile of v1, /device:TPU:2, one launch (start us, length us, event | category | flops | bytes accessed | tf_op | source)
XLA Modules:
  0.0 513.6 jit_solution(2242039293671178522)
XLA Ops:
  7.3 2.2 convert_element_type.38
  9.5 0.7 fusion.15
  10.2 18.0 %reduce-window.6 = s32[64,8,128]{2,1,0:T(8,128)S(1)} reduce-window(s32[64,8,128]{2,1,0:T(8,128)S(1)} %fusion.15, s32[]{:T(128)} %constant.18.clone.1), window={size=1x1x128 pad=0_0x0_0x127_0}, to_apply=%region_0.1 | reduce-window | flops 8323072 | bytes 524292 | tf_op jit(solution)/shard_map/reduce-window
  28.7 0.7 fusion.16
  29.4 3.9 gather_fusion
  33.5 0.4 fusion.18
  33.9 6.0 %scatter_custom_fusion = bf16[2048,256]{1,0:T(8,128)(2,1)S(1)} fusion(s32[1024]{0:T(1024)S(1)} %bitcast.71, bf16[]{:T(256)} %constant.22.clone.1, f32[1024,256]{1,0:T(8,128)S(1)} %fusion.18, f32[]{:T(128)} %constant.15.clone.1, bf16[1024,256]{1,0:T(8,128)(2,1)S(1)} %gather_fusion, pred[1024]{0:T(1024)(128)(4,1)S(1)} %compare_and_fusion), kind=kCustom, calls=%fused_computation.32 | custom fusion | flops 2097152 | bytes 2622470 | tf_op jit(solution)/shard_map/scatter | solution.py:85
  39.9 40.8 %all_to_all.20 = bf16[64,32,256]{2,1,0:T(8,128)(2,1)S(1)} all-to-all(bf16[64,32,256]{2,1,0:T(8,128)(2,1)S(1)} %bitcast.65), channel_id=1, replica_groups=mesh['dp'=4,'expert'=64] {'expert'}, dimensions={0} | all-to-all | bytes 2097152 | tf_op jit(solution)/shard_map/all_to_all | solution.py:90
  80.7 9.8 %multiply_convert_fusion.1 = (bf16[2048,2048]{1,0:T(8,128)(2,1)S(1)}, f32[2048,2048]{1,0:T(8,128)}) fusion(bf16[2048,256]{1,0:T(8,128)(2,1)S(1)} %bitcast.60, bf16[1,2,256,2048]{3,2,1,0:T(8,128)(2,1)} %all-gather.4.cloned.1.call-done), kind=kOutput, calls=%fused_computation.6 | convolution fusion | flops 2168455168 | bytes 27262976 | tf_op jit(solution)/shard_map/dot_general | solution.py:20
  90.5 3.2 copy-done.2
  93.7 3.8 fusion.1
  97.5 5.6 %all-to-all-start.1 = ((f32[64,32,256]{2,1,0:T(8,128)}), f32[64,32,256]{2,1,0:T(8,128)S(1)}, u32[]{:S(2)}, u32[]{:S(2)}) async-start(f32[64,32,256]{2,1,0:T(8,128)} %fusion.1), calls=%async_computation.1 | async-start | bytes 4194304 | tf_op jit(solution)/shard_map/all_to_all | solution.py:94
  103.1 0.2 reduce-scatter.2.cloned.1.call-start
  103.4 51.1 %all-to-all-done.1 = f32[64,32,256]{2,1,0:T(8,128)S(1)} async-done(((f32[64,32,256]{2,1,0:T(8,128)}), f32[64,32,256]{2,1,0:T(8,128)S(1)}, u32[]{:S(2)}, u32[]{:S(2)}) %all-to-all-start.1) | async-done | bytes 2097184 | tf_op jit(solution)/shard_map/all_to_all | solution.py:94
  154.5 3.5 gather_fusion.1
  158.0 5.9 %scatter_custom_fusion.1 = bf16[2048,256]{1,0:T(8,128)(2,1)S(1)} fusion(s32[1024]{0:T(1024)S(1)} %bitcast.73, f32[1024,256]{1,0:T(8,128)S(1)} %gather_fusion.1, bf16[1024,256]{1,0:T(8,128)(2,1)} %param.11, f32[]{:T(128)} %constant.16.clone.1, bf16[]{:T(256)} %constant.22.clone.1), kind=kCustom, calls=%fused_computation.29 | custom fusion | flops 1048576 | bytes 2621446 | tf_op jit(solution)/shard_map/scatter | solution.py:85
  163.9 34.0 %all_to_all.21 = bf16[64,32,256]{2,1,0:T(8,128)(2,1)S(1)} all-to-all(bf16[64,32,256]{2,1,0:T(8,128)(2,1)S(1)} %bitcast.64), channel_id=1, replica_groups=mesh['dp'=4,'expert'=64] {'expert'}, dimensions={0} | all-to-all | bytes 2097152 | tf_op jit(solution)/shard_map/all_to_all | solution.py:102
  197.9 5.9 %convolution_bitcast_fusion = f32[1,256,2048]{2,1,0:T(8,128)S(1)} fusion(bf16[2048,256]{1,0:T(8,128)(2,1)S(1)} %bitcast.62, bf16[2048,2048]{1,0:T(8,128)(2,1)} %copy-done.2), kind=kOutput, calls=%fused_computation.9 | convolution fusion | flops 2147483648 | bytes 11534336 | tf_op jit(solution)/shard_map/dot_general | solution.py:29
  203.9 10.4 %multiply_convert_fusion = bf16[2048,2048]{1,0:T(8,128)(2,1)S(1)} fusion(f32[2048,2048]{1,0:T(8,128)} %get-tuple-element.9, bf16[2048,256]{1,0:T(8,128)(2,1)S(1)} %bitcast.63, bf16[1,2,256,2048]{3,2,1,0:T(8,128)(2,1)S(1)} %copy-done.17), kind=kOutput, calls=%fused_computation.5 | convolution fusion | flops 2185232384 | bytes 27262976 | tf_op jit(solution)/shard_map/dot_general | solution.py:32
  214.2 3.2 copy-done.3
  217.5 2.4 convolution_bitcast_fusion.1
  219.8 2.3 maximum_bitcast_fusion
  222.1 0.3 all-gather.6.cloned.1.call-start
  222.4 6.0 %convolution_convert_fusion = bf16[2048,256]{1,0:T(8,128)(2,1)S(1)} fusion(bf16[2048,2048]{1,0:T(8,128)(2,1)} %copy-done.3, bf16[1,2,256,2048]{3,2,1,0:T(8,128)(2,1)} %all-gather.4.cloned.1.call-done), kind=kOutput, calls=%fused_computation.11 | convolution fusion | flops 2148007936 | bytes 10485760 | tf_op jit(solution)/shard_map/dot_general | solution.py:37
  228.4 34.4 %all_to_all.22 = bf16[64,32,256]{2,1,0:T(8,128)(2,1)S(1)} all-to-all(bf16[64,32,256]{2,1,0:T(8,128)(2,1)S(1)} %bitcast.66), channel_id=1, replica_groups=mesh['dp'=4,'expert'=64] {'expert'}, dimensions={0} | all-to-all | bytes 2097152 | tf_op jit(solution)/shard_map/all_to_all | solution.py:108
  262.8 5.0 gather_fusion.2
  267.8 2.9 fusion.12
  270.7 0.2 multiply_reduce_fusion
  271.0 0.6 broadcast_multiply_fusion
  271.6 4.0 divide_subtract_fusion
  275.6 209.7 %all-gather.6.cloned.1.call-done = f32[65536,256]{1,0:T(8,128)} async-done(((f32[256,256]{1,0:T(8,128)}), f32[65536,256]{1,0:T(8,128)}) %all-gather.6.cloned.1.call-update) | async-done | bytes 67108880 | tf_op jit(solution)/shard_map/all_gather | solution.py:120
  485.2 21.8 %reduce_sum.28 = f32[256,256]{1,0:T(8,128)} reduce(f32[256,256,256]{2,1,0:T(8,128)} %bitcast.17, f32[]{:T(128)} %constant.17.clone.1), dimensions={0}, to_apply=%region_5.6 | reduce | flops 16711680 | bytes 67371008 | tf_op jit(solution)/shard_map/reduce_sum | solution.py:120
  (51 shorter events, 0.8 us)
Async XLA Ops:
  7.2 22.3 %copy-start = (bf16[2048,256]{1,0:T(8,128)(2,1)S(1)}, bf16[2048,256]{1,0:T(8,128)(2,1)}, u32[]{:S(2)}) copy-start(bf16[2048,256]{1,0:T(8,128)(2,1)} %param.8) | copy-start | bytes 3145732
  7.2 26.2 %copy-start.14 = (s32[1024,1]{0,1:T(1,128)S(1)}, s32[1024,1]{0,1:T(1,128)}, u32[]{:S(2)}) copy-start(s32[1024,1]{0,1:T(1,128)} %param.10) | copy-start | bytes 12292
  7.2 26.3 %copy-start.15 = (s32[1024]{0:T(1024)S(1)}, s32[1024]{0:T(1024)}, u32[]{:S(2)}) copy-start(s32[1024]{0:T(1024)} %param.9) | copy-start | bytes 12292
  7.2 26.3 %copy-start.13 = (bf16[256,256]{1,0:T(8,128)(2,1)S(1)}, bf16[256,256]{1,0:T(8,128)(2,1)}, u32[]{:S(2)}) copy-start(bf16[256,256]{1,0:T(8,128)(2,1)} %param.12) | copy-start | bytes 393220
  7.2 73.5 %all-gather.4.cloned.1.call-start = ((), (), s32[]{:S(2)}) async-start(), calls=%async_computation.5 | async-start | bytes 2621440 | tf_op jit(solution)/shard_map/all_gather | solution.py:87
  33.4 57.1 %copy-start.8 = (bf16[1024,256]{1,0:T(8,128)(2,1)}, bf16[1024,256]{1,0:T(8,128)(2,1)S(1)}, u32[]{:S(2)}) copy-start(bf16[1024,256]{1,0:T(8,128)(2,1)S(1)} %gather_fusion) | copy-start | bytes 1572868
  33.9 6.0 %copy-start.11 = (f32[1024,256]{1,0:T(8,128)}, f32[1024,256]{1,0:T(8,128)S(1)}, u32[]{:S(2)}) copy-start(f32[1024,256]{1,0:T(8,128)S(1)} %fusion.18) | copy-start | bytes 3145732
  80.7 9.8 %copy-start.6 = (bf16[64,32,256]{2,1,0:T(8,128)(2,1)}, bf16[64,32,256]{2,1,0:T(8,128)(2,1)S(1)}, u32[]{:S(2)}) copy-start(bf16[64,32,256]{2,1,0:T(8,128)(2,1)S(1)} %all_to_all.20) | copy-start | bytes 3145732
  80.7 13.0 %copy-start.16 = (bf16[1,2,256,2048]{3,2,1,0:T(8,128)(2,1)S(1)}, bf16[1,2,256,2048]{3,2,1,0:T(8,128)(2,1)}, u32[]{:S(2)}) copy-start(bf16[1,2,256,2048]{3,2,1,0:T(8,128)(2,1)} %all-gather.4.cloned.1.call-done) | copy-start | bytes 6291460
  90.5 3.2 copy-start.2
  97.5 56.9 %all-to-all-start.1 = ((f32[64,32,256]{2,1,0:T(8,128)}), f32[64,32,256]{2,1,0:T(8,128)S(1)}, u32[]{:S(2)}, u32[]{:S(2)}) async-start(f32[64,32,256]{2,1,0:T(8,128)} %fusion.1), calls=%async_computation.1 | async-start | bytes 4194304 | tf_op jit(solution)/shard_map/all_to_all | solution.py:94
  103.1 168.4 %reduce-scatter.2.cloned.1.call-start = ((), (), s32[]{:S(2)}) async-start(), calls=%async_computation.6 | async-start | bytes 5242880 | tf_op jit(solution)/shard_map/reduce_scatter | solution.py:122
  157.9 45.9 %copy-start.4 = (f32[1024,256]{1,0:T(8,128)}, f32[1024,256]{1,0:T(8,128)S(1)}, u32[]{:S(2)}) copy-start(f32[1024,256]{1,0:T(8,128)S(1)} %gather_fusion.1) | copy-start | bytes 3145732
  197.9 5.9 %copy-start.17 = (bf16[1,2,256,2048]{3,2,1,0:T(8,128)(2,1)S(1)}, bf16[1,2,256,2048]{3,2,1,0:T(8,128)(2,1)}, u32[]{:S(2)}) copy-start(bf16[1,2,256,2048]{3,2,1,0:T(8,128)(2,1)} %all-gather.4.cloned.1.call-done) | copy-start | bytes 6291460
  203.8 13.6 %copy-start.7 = (bf16[64,32,256]{2,1,0:T(8,128)(2,1)S(1)}, bf16[64,32,256]{2,1,0:T(8,128)(2,1)}, u32[]{:S(2)}) copy-start(bf16[64,32,256]{2,1,0:T(8,128)(2,1)} %copy-done.6) | copy-start | bytes 3145732
  214.2 3.2 copy-start.3
  222.1 45.7 %copy-start.9 = (bf16[1024,256]{1,0:T(8,128)(2,1)S(1)}, bf16[1024,256]{1,0:T(8,128)(2,1)}, u32[]{:S(2)}) copy-start(bf16[1024,256]{1,0:T(8,128)(2,1)} %copy-done.8) | copy-start | bytes 1572868
  222.1 263.1 %all-gather.6.cloned.1.call-start = ((), (), s32[]{:S(2)}) async-start(), calls=%async_computation.7 | async-start | bytes 67371008 | tf_op jit(solution)/shard_map/all_gather | solution.py:120
  228.4 42.3 %copy-start.5 = (f32[1024,256]{1,0:T(8,128)S(1)}, f32[1024,256]{1,0:T(8,128)}, u32[]{:S(2)}) copy-start(f32[1024,256]{1,0:T(8,128)} %copy-done.4) | copy-start | bytes 3145732
  228.4 42.3 %copy-start.12 = (bf16[1024,256]{1,0:T(8,128)(2,1)S(1)}, bf16[1024,256]{1,0:T(8,128)(2,1)}, u32[]{:S(2)}) copy-start(bf16[1024,256]{1,0:T(8,128)(2,1)} %param.11) | copy-start | bytes 1572868
  267.8 3.8 copy-start.10
  485.2 21.8 %copy-start.1 = (bf16[2048,256]{1,0:T(8,128)(2,1)S(1)}, bf16[2048,256]{1,0:T(8,128)(2,1)}, u32[]{:S(2)}) copy-start(bf16[2048,256]{1,0:T(8,128)(2,1)} %param.8) | copy-start | bytes 3145732
Sparse Core Ops, SparseCore 0:
  10.4 35.3 all-gather.3
  222.2 44.4 reduce-scatter.1
  271.7 213.4 all-gather.5
